TPU v7x, 32 devices: a whole 2x2x4 slice. The times are simulated.
32 devices in a mesh: dp: 8 (over z, x), seq: 4 (over y, core).
Axes of the slice: x: 2, y: 2, z: 4, core: 2. Of those that a mesh axis runs over, the one named last changes fastest.
Arguments:
- layer_in: bfloat16 [8192, 2048], P(('dp', 'seq')), may hold values from -6 to 6
- out_grad: bfloat16 [8192, 2048], P(('dp', 'seq')), may hold values from -6 to 6
- seq_start: int32 [8, 4], P('dp'), may hold values from 0 to 1, as said below
- norm1_gain: bfloat16 [2048], P(('dp', 'seq')), may hold values from 0.25 to 1.75
- norm1_shift: bfloat16 [2048], P(('dp', 'seq')), may hold values from -3 to 3
- proj_in: bfloat16 [2048, 12288], P(('dp', 'seq')), may hold values from -0.125 to 0.125
- proj_out: bfloat16 [4096, 2048], P(('dp', 'seq')), may hold values from -0.125 to 0.125
- norm2_gain: bfloat16 [2048], P(('dp', 'seq')), may hold values from 0.25 to 1.75
- norm2_shift: bfloat16 [2048], P(('dp', 'seq')), may hold values from -3 to 3
- ffn_up: bfloat16 [2048, 4096], P(('dp', 'seq')), may hold values from -0.125 to 0.125
- ffn_down: bfloat16 [4096, 2048], P(('dp', 'seq')), may hold values from -0.125 to 0.125
Outputs:
- layer_out: bfloat16 [8192, 2048], P(('dp', 'seq'))
- in_grad: bfloat16 [8192, 2048], P(('dp', 'seq'))
- norm1_gain_grad: float32 [2048], P(('dp', 'seq'))
- norm1_shift_grad: float32 [2048], P(('dp', 'seq'))
- proj_in_grad: float32 [2048, 12288], P(('dp', 'seq'))
- proj_out_grad: float32 [4096, 2048], P(('dp', 'seq'))
- norm2_gain_grad: float32 [2048], P(('dp', 'seq'))
- norm2_shift_grad: float32 [2048], P(('dp', 'seq'))
- ffn_up_grad: float32 [2048, 4096], P(('dp', 'seq'))
- ffn_down_grad: float32 [4096, 2048], P(('dp', 'seq'))
Inputs may be any that keep to these rules, and one draw needn't show every extreme that they name: `seq_start`: each group's first block is 1, and a 1 stands only at even block indices, so every sequence covers an even number of blocks of 256 tokens.
All inputs are finite; a program needn't handle non-finite values.
Results may differ from a plain program's by a relative error of at most 0.014.
The roundings to bfloat16 on the way count: a program that leaves them out, or rounds other values in their place, can miss the bound.
Values may be sent and summed in bfloat16 or wider, within the bound.
No kernel may reach another device: no remote copies, remote signals or barrier semaphores. Data moves between devices by JAX's collectives and lax.ppermute only.
A program may use at most 336 MiB of HBM per device.

v0:
```python
import jax
import jax.numpy as jnp
from jax import lax
from jax.sharding import PartitionSpec as P

D = 2048
HEADS = 8
VD = 4096
DK = 256
DV = 512
BOTH = ("dp", "seq")
f32 = jnp.float32
bf16 = jnp.bfloat16


def layer_norm(rows, row_gain, row_shift):
    average = jnp.mean(rows, axis=-1, keepdims=True)
    centred = rows - average
    spread = jnp.mean(centred * centred, axis=-1, keepdims=True)
    return centred * lax.rsqrt(spread + 1e-05) * row_gain + row_shift


def gate_norm(gate_pre, retained):
    average = jnp.mean(retained, axis=-1, keepdims=True)
    centred = retained - average
    spread = jnp.maximum(jnp.mean(centred * centred, axis=-1, keepdims=True), 0.25)
    normed = centred * lax.rsqrt(spread + 1e-05)
    swish = gate_pre * jax.nn.sigmoid(gate_pre)
    return swish * normed


def gelu_exact(values):
    return jax.nn.gelu(values, approximate=False)


def rotate(heads_in, cosine, sine):
    half_width = heads_in.shape[-1] // 2
    first = heads_in[..., :half_width]
    second = heads_in[..., half_width:]
    return jnp.concatenate(
        [first * cosine - second * sine, first * sine + second * cosine], axis=-1
    )


def dot(a, b, dims):
    return lax.dot_general(a, b, (dims, ((), ())), preferred_element_type=f32)


def seq_bits(size):
    return [1 << b for b in range(size.bit_length() - 1)]


def swap_seq(x, bit):
    size = lax.axis_size("seq")
    return lax.ppermute(x, "seq", [(i, i ^ bit) for i in range(size)])


def gather_seq(x):
    size, me = (lax.axis_size("seq"), lax.axis_index("seq"))
    held = x[None]
    for bit in reversed(seq_bits(size)):
        other = swap_seq(held, bit)
        upper = me & bit != 0
        held = jnp.where(upper, jnp.stack([other, held]), jnp.stack([held, other]))
        held = held.reshape((-1,) + x.shape) if bit == size // 2 else held
        if bit != size // 2:
            held = jnp.swapaxes(held, 0, 1).reshape((-1,) + x.shape)
    return held


def scatter_seq(x):
    size, me = (lax.axis_size("seq"), lax.axis_index("seq"))
    held = x
    for bit in seq_bits(size):
        pairs = held.reshape((held.shape[0] // 2, 2) + held.shape[1:])
        mine = jnp.where(me & bit != 0, 1, 0)
        keep = lax.dynamic_index_in_dim(pairs, mine, 1, False)
        give = lax.dynamic_index_in_dim(pairs, 1 - mine, 1, False)
        held = keep.astype(f32) + swap_seq(give.astype(bf16), bit).astype(f32)
    return held[0]


def exchange_seq(x):
    return lax.all_to_all(x, "seq", 0, 0)


def gather_dp(x):
    return lax.all_gather(x, "dp", axis=0, tiled=True)


def scatter_dp(x):
    return lax.psum_scatter(x.astype(bf16), "dp", scatter_dimension=0, tiled=True)


def local(
    layer_in,
    out_grad,
    seq_start,
    norm1_gain,
    norm1_shift,
    proj_in,
    proj_out,
    norm2_gain,
    norm2_shift,
    ffn_up,
    ffn_down,
):
    S, G = (lax.axis_size("seq"), lax.axis_size("dp"))
    me = lax.axis_index("seq")
    T = layer_in.shape[0]
    TG = S * T
    H = HEADS // S
    QW, VW = (H * DK, H * DV)
    FR = ffn_down.shape[0]
    FW = G * FR
    norms = lax.all_gather(
        jnp.stack([norm1_gain, norm1_shift, norm2_gain, norm2_shift]), BOTH, axis=1, tiled=True
    ).astype(f32)
    gain_one, shift_one, gain_two, shift_two = norms
    rows_in = proj_in.shape[0]
    pieces = []
    start = 0
    for width in (QW, QW, VW, VW):
        part = proj_in[:, start : start + S * width]
        pieces.append(part.reshape(rows_in, S, width))
        start += S * width
    w_in = jnp.concatenate(pieces, axis=2).transpose(1, 0, 2)
    w_in = exchange_seq(w_in).reshape(S * rows_in, 2 * QW + 2 * VW)
    w_in = gather_dp(w_in)
    w_out = lax.ppermute(
        proj_out, BOTH, [(j * G + t, t * S + j) for j in range(S) for t in range(G)]
    )
    w_out = gather_dp(w_out)
    rows_up = ffn_up.shape[0]
    w_up = ffn_up.reshape(rows_up, G, S, FR).transpose(2, 0, 1, 3).reshape(S, rows_up, FW)
    w_up = gather_dp(exchange_seq(w_up).reshape(S * rows_up, FW))
    w_down = gather_dp(ffn_down)
    rows_full = layer_in.astype(f32)
    normed_one, norm1_back = jax.vjp(layer_norm, rows_full, gain_one, shift_one)
    hidden_one = gather_seq(normed_one.astype(bf16)).reshape(TG, D)
    cot = gather_seq(out_grad).reshape(TG, D)
    projected = dot(hidden_one, w_in, ((1,), (0,)))
    q_pre = projected[:, :QW].reshape(S, T, H, DK)
    k_pre = projected[:, QW : 2 * QW].reshape(S, T, H, DK)
    values = projected[:, 2 * QW : 2 * QW + VW].astype(bf16).reshape(S, T, H, DV)
    gate_pre = projected[:, 2 * QW + VW :].reshape(S, T, H, DV)
    half = DK // 2
    factor = jnp.power(10000.0, -jnp.arange(half, dtype=f32) / (half - 1))
    angles = jnp.arange(TG, dtype=f32)[:, None] * factor[None, :]
    cosine = jnp.cos(angles).reshape(S, T, 1, half)
    sine = jnp.sin(angles).reshape(S, T, 1, half)
    key_scale = DK ** (-0.5)
    queries = rotate(q_pre, cosine, sine).astype(bf16)
    keys = (rotate(k_pre, cosine, sine) * key_scale).astype(bf16)
    log_all = jnp.log(1.0 - jnp.exp2(-5.0 - jnp.arange(HEADS, dtype=f32)))
    log_decay = lax.dynamic_slice_in_dim(log_all, me * H, H)
    steps = jnp.arange(T, dtype=f32)
    decay_query = jnp.exp((steps + 1.0)[:, None] * log_decay[None, :])
    decay_key = jnp.exp((T - 1.0 - steps)[:, None] * log_decay[None, :])
    distance = steps[:, None] - steps[None, :]
    lower = distance[None] >= 0.0
    safe = jnp.where(lower, distance[None], 0.0)
    mask = jnp.where(lower, jnp.exp(safe * log_decay[:, None, None]), 0.0)
    block_decay = jnp.exp(T * log_decay)[:, None, None]
    keep = 1.0 - seq_start[0].astype(f32)
    query_decay = (queries.astype(f32) * decay_query[None, :, :, None]).astype(bf16)
    key_decay = (keys.astype(f32) * decay_key[None, :, :, None]).astype(bf16)

    def ein(spec, a, b):
        return jnp.einsum(spec, a, b, preferred_element_type=f32)

    raw = ein("bihd,bjhd->bhij", queries, keys)
    scores = (raw * mask[None]).astype(bf16)
    local_state = ein("bjhd,bjhe->bhde", key_decay, values)
    carry = jnp.zeros_like(local_state[0])
    states = []
    for b in range(S):
        state = keep[b] * carry
        states.append(state.astype(bf16))
        carry = block_decay * state + local_state[b]
    state_in = jnp.stack(states)
    retained = ein("bhij,bjhe->bihe", scores, values) + ein(
        "bihd,bhde->bihe", query_decay, state_in
    )
    gated, gate_back = jax.vjp(gate_norm, gate_pre, retained)
    mixed = gated.astype(bf16).reshape(TG, VW)
    attn = scatter_seq(dot(mixed, w_out, ((1,), (0,))).reshape(S, T, D))
    middle = rows_full + attn
    normed_two, norm2_back = jax.vjp(layer_norm, middle, gain_two, shift_two)
    hidden_two = gather_seq(normed_two.astype(bf16)).reshape(TG, D)
    up_pre = dot(hidden_two, w_up, ((1,), (0,)))
    active_full, gelu_back = jax.vjp(gelu_exact, up_pre)
    active = active_full.astype(bf16)
    down = scatter_seq(dot(active, w_down, ((1,), (0,))).reshape(S, T, D))
    layer_out = (middle + down).astype(bf16)
    down_grad = scatter_dp(dot(active, cot, ((0,), (0,)))).astype(f32)
    grad_active = dot(cot, w_down, ((1,), (1,)))
    grad_up = gelu_back(grad_active)[0].astype(bf16)
    up_grad = scatter_dp(dot(hidden_two, grad_up, ((0,), (0,))))
    up_grad = exchange_seq(up_grad.reshape(S, rows_up, FW)).reshape(S, rows_up, G, FR)
    up_grad = up_grad.transpose(1, 2, 0, 3).reshape(rows_up, G * S * FR).astype(f32)
    grad_hidden_two = scatter_seq(dot(grad_up, w_up, ((1,), (1,))).reshape(S, T, D))
    grad_mid_part, gain_two_grad, shift_two_grad = norm2_back(grad_hidden_two)
    grad_middle = out_grad.astype(f32) + grad_mid_part
    grad_attn = gather_seq(grad_middle.astype(bf16)).reshape(TG, D)
    out_term = scatter_dp(dot(mixed, grad_attn, ((0,), (0,))))
    out_grad_w = lax.ppermute(
        out_term, BOTH, [(t * S + j, j * G + t) for j in range(S) for t in range(G)]
    ).astype(f32)
    grad_mixed = dot(grad_attn, w_out, ((1,), (1,))).reshape(S, T, H, DV)
    grad_gate, grad_ret = gate_back(grad_mixed)
    grad_gate = grad_gate.astype(bf16)
    grad_ret = grad_ret.astype(bf16)
    grad_qdecay = ein("bihe,bhde->bihd", grad_ret, state_in)
    state_grad = ein("bihd,bihe->bhde", query_decay, grad_ret)
    grad_scores = ein("bihe,bjhe->bhij", grad_ret, values)
    grad_raw = (grad_scores * mask[None]).astype(bf16)
    later = jnp.zeros_like(state_grad[0])
    laters = [None] * S
    for b in reversed(range(S)):
        laters[b] = later.astype(bf16)
        later = keep[b] * (state_grad[b] + block_decay * later)
    grad_local = jnp.stack(laters)
    grad_query = (
        ein("bhij,bjhd->bihd", grad_raw, keys) + grad_qdecay * decay_query[None, :, :, None]
    )
    grad_key = (
        ein("bhij,bihd->bjhd", grad_raw, queries)
        + ein("bjhe,bhde->bjhd", values, grad_local) * decay_key[None, :, :, None]
    )
    grad_value = ein("bhij,bihe->bjhe", scores, grad_ret) + ein(
        "bjhd,bhde->bjhe", key_decay, grad_local
    )
    grad_qpre = rotate(grad_query, cosine, -sine).astype(bf16).reshape(TG, QW)
    grad_kpre = rotate(grad_key * key_scale, cosine, -sine).astype(bf16).reshape(TG, QW)
    grad_projected = jnp.concatenate(
        [grad_qpre, grad_kpre, grad_value.astype(bf16).reshape(TG, VW), grad_gate.reshape(TG, VW)],
        axis=1,
    )
    in_term = scatter_dp(dot(hidden_one, grad_projected, ((0,), (0,))))
    in_term = exchange_seq(in_term.reshape(S, rows_in, 2 * QW + 2 * VW))
    cols = []
    start = 0
    for width in (QW, QW, VW, VW):
        part = in_term[:, :, start : start + width]
        cols.append(part.transpose(1, 0, 2).reshape(rows_in, S * width))
        start += width
    in_grad_w = jnp.concatenate(cols, axis=1).astype(f32)
    grad_hidden_one = scatter_seq(dot(grad_projected, w_in, ((1,), (1,))).reshape(S, T, D))
    grad_in_part, gain_one_grad, shift_one_grad = norm1_back(grad_hidden_one)
    in_grad = (grad_middle + grad_in_part).astype(bf16)
    norm_grads = lax.psum_scatter(
        jnp.stack([gain_one_grad, shift_one_grad, gain_two_grad, shift_two_grad]),
        BOTH,
        scatter_dimension=1,
        tiled=True,
    )
    return (
        layer_out,
        in_grad,
        norm_grads[0],
        norm_grads[1],
        in_grad_w,
        out_grad_w,
        norm_grads[2],
        norm_grads[3],
        up_grad,
        down_grad,
    )


def solution(mesh):
    rows, vector = (P(BOTH, None), P(BOTH))
    in_specs = (rows, rows, P("dp", None), vector, vector, rows, rows, vector, vector, rows, rows)
    out_specs = (rows, rows, vector, vector, rows, rows, vector, vector, rows, rows)
    return jax.shard_map(local, mesh=mesh, in_specs=in_specs, out_specs=out_specs, check_vma=False)
```

profile of v0, /device:TPU:0, one launch (start us, length us, event | category | flops | bytes accessed | tf_op | source)
XLA Modules:
  0.0 1129.7 jit_solution(7035085313268230148)
XLA Ops:
  12.0 24.4 %all_to_all.20 = bf16[4,64,3072]{2,1,0:T(8,128)(2,1)} all-to-all(bf16[4,64,3072]{2,1,0:T(8,128)(2,1)S(1)} %copy.198), channel_id=1, replica_groups=mesh['dp'=8,'seq'=4] {'seq'}, dimensions={0} | all-to-all | bytes 3145728 | tf_op jit(solution)/shard_map/all_to_all | solution.py:84
  38.0 106.0 %all-gather = bf16[32,64,4]{1,2,0:T(4,128)(2,1)S(1)} all-gather(bf16[1,64,4]{1,2,0:T(4,128)(2,1)S(1)} %maximum_bitcast_fusion.1), channel_id=1, replica_groups=mesh['dp'=8,'seq'=4] {'dp','seq'}, dimensions={0}, use_global_device_ids=true | all-gather | bytes 16896 | tf_op jit(solution)/shard_map/all_gather | solution.py:116
  153.1 4.1 all-to-all-start.1
  157.3 15.8 %collective-permute-done = bf16[1,256,2048]{2,1,0:T(8,128)(2,1)S(1)} collective-permute-done((bf16[1,256,2048]{2,1,0:T(8,128)(2,1)}, bf16[1,256,2048]{2,1,0:T(8,128)(2,1)S(1)}, u32[]{:S(2)}, u32[]{:S(2)}) %collective-permute-start) | collective-permute-done | bytes 1048608 | tf_op jit(solution)/shard_map/ppermute | solution.py:55
  173.1 3.3 maximum_select_fusion.4
  179.5 3.1 fusion.58
  183.3 2.8 fusion.4
  186.1 2.3 copy.197
  188.4 51.1 %all-gather.6.cloned.1.call-done = bf16[2048,3072]{1,0:T(8,128)(2,1)} async-done(((bf16[256,3072]{1,0:T(8,128)(2,1)}), bf16[2048,3072]{1,0:T(8,128)(2,1)}) %all-gather.6.cloned.1.call-update) | async-done | bytes 12582928 | tf_op jit(solution)/shard_map/all_gather | solution.py:88
  239.5 17.0 %fusion.85 = f32[1024,3072]{1,0:T(8,128)S(1)} fusion(bf16[1024,2048]{1,0:T(8,128)(2,1)} %bitcast.265, bf16[2048,3072]{1,0:T(8,128)(2,1)} %all-gather.6.cloned.1.call-done), kind=kOutput, calls=%fused_computation.220 | convolution fusion | flops 12884901888 | bytes 29360128 | tf_op jit(solution)/shard_map/dot_general | solution.py:46
  260.4 2.4 fusion.77
  262.8 3.3 reshape.733
  266.1 4.3 reshape.734
  270.5 6.7 reshape.732
  277.2 7.2 copy.200
  284.4 3.7 reshape.735
  288.1 2.6 fusion.78
  292.6 2.5 fusion.68
  303.1 10.7 all-gather.8.cloned.1.call-done
  313.8 6.4 fusion.8
  324.2 4.4 collective-permute-done.3
  328.5 2.8 bitcast_add_fusion.3
  335.7 23.9 %collective-permute-done.4 = bf16[1,256,2048]{2,1,0:T(8,128)(2,1)} collective-permute-done((bf16[1,256,2048]{2,1,0:T(8,128)(2,1)S(1)}, bf16[1,256,2048]{2,1,0:T(8,128)(2,1)}, u32[]{:S(2)}, u32[]{:S(2)}) %collective-permute-start.4) | collective-permute-done | bytes 1048608 | tf_op jit(solution)/shard_map/ppermute | solution.py:55
  359.7 2.3 fusion.76
  364.4 17.7 %collective-permute-done.9 = bf16[1,256,2048]{2,1,0:T(8,128)(2,1)S(1)} collective-permute-done((bf16[1,256,2048]{2,1,0:T(8,128)(2,1)}, bf16[1,256,2048]{2,1,0:T(8,128)(2,1)S(1)}, u32[]{:S(2)}, u32[]{:S(2)}) %collective-permute-start.9) | collective-permute-done | bytes 1048608 | tf_op jit(solution)/shard_map/ppermute | solution.py:55
  384.1 19.6 %collective-permute-done.5 = bf16[1,256,2048]{2,1,0:T(8,128)(2,1)S(1)} collective-permute-done((bf16[1,256,2048]{2,1,0:T(8,128)(2,1)S(1)}, bf16[1,256,2048]{2,1,0:T(8,128)(2,1)S(1)}, u32[]{:S(2)}, u32[]{:S(2)}) %collective-permute-start.5) | collective-permute-done | bytes 1048608 | tf_op jit(solution)/shard_map/ppermute | solution.py:55
  411.0 2.3 copy.210
  413.4 9.9 fusion.86
  423.2 38.1 %all-gather.12.cloned.1.call-done = bf16[1024,2048]{1,0:T(8,128)(2,1)} async-done(((bf16[128,2048]{1,0:T(8,128)(2,1)}), bf16[1024,2048]{1,0:T(8,128)(2,1)}) %all-gather.12.cloned.1.call-update) | async-done | bytes 4194320 | tf_op jit(solution)/shard_map/all_gather | solution.py:88
  461.3 16.9 %add_convert_fusion.2 = (bf16[1024,1024]{1,0:T(8,128)(2,1)S(1)}, f32[1024,1024]{1,0:T(8,128)S(1)}) fusion(f32[1024,1024]{1,0:T(8,128)} %fusion.86, bf16[1024,2048]{1,0:T(8,128)(2,1)} %bitcast.269, bf16[1024,2048]{1,0:T(8,128)(2,1)} %all-gather.12.cloned.1.call-done), kind=kOutput, calls=%fused_computation.31 | convolution fusion | flops 4370464768 | bytes 18874368 | tf_op jit(solution)/shard_map/dot_general | solution.py:46
  478.2 2.5 multiply_convert_fusion
  481.9 6.2 convolution_convert_fusion.2
  488.2 7.3 fusion.88
  497.1 4.5 fusion.87
  506.3 2.5 bitcast_add_fusion.2
  510.5 18.6 %collective-permute-done.12 = bf16[1,256,2048]{2,1,0:T(8,128)(2,1)S(1)} collective-permute-done((bf16[1,256,2048]{2,1,0:T(8,128)(2,1)S(1)}, bf16[1,256,2048]{2,1,0:T(8,128)(2,1)S(1)}, u32[]{:S(2)}, u32[]{:S(2)}) %collective-permute-start.12) | collective-permute-done | bytes 1048608 | tf_op jit(solution)/shard_map/ppermute | solution.py:55
  529.9 21.3 %collective-permute-done.8 = bf16[1,256,2048]{2,1,0:T(8,128)(2,1)S(1)} collective-permute-done((bf16[1,256,2048]{2,1,0:T(8,128)(2,1)S(1)}, bf16[1,256,2048]{2,1,0:T(8,128)(2,1)S(1)}, u32[]{:S(2)}, u32[]{:S(2)}) %collective-permute-start.8) | collective-permute-done | bytes 1048608 | tf_op jit(solution)/shard_map/ppermute | solution.py:55
  553.1 2.4 fusion.124
  557.0 23.3 %collective-permute-done.13 = bf16[1,256,2048]{2,1,0:T(8,128)(2,1)S(1)} collective-permute-done((bf16[1,256,2048]{2,1,0:T(8,128)(2,1)S(1)}, bf16[1,256,2048]{2,1,0:T(8,128)(2,1)S(1)}, u32[]{:S(2)}, u32[]{:S(2)}) %collective-permute-start.13) | collective-permute-done | bytes 1048608 | tf_op jit(solution)/shard_map/ppermute | solution.py:55
  582.1 6.4 convolution_convert_fusion.1
  592.0 3.0 fusion.7
  595.8 3.0 copy-done.1
  600.1 5.3 multiply_reduce_fusion
  605.4 4.6 fusion.73
  610.0 6.6 copy.235
  616.6 3.7 copy.281
  622.4 2.6 fusion.48
  635.7 2.4 fusion.37
  638.1 6.3 copy.232
  648.8 3.2 copy-done.48
  653.1 16.0 %convolution_convert_fusion = bf16[2048,3072]{1,0:T(8,128)(2,1)} fusion(bf16[1024,2048]{1,0:T(8,128)(2,1)S(1)} %bitcast.266, bf16[1024,3072]{1,0:T(8,128)(2,1)S(1)} %constant_dynamic-update-slice_fusion), kind=kOutput, calls=%fused_computation | convolution fusion | flops 12891193344 | bytes 23068672 | tf_op jit(solution)/shard_map/dot_general | solution.py:46
  669.2 6.2 copy.241
  678.2 6.2 convolution_convert_fusion.3
  684.4 18.0 %fusion.90 = f32[1024,2048]{1,0:T(8,128)S(1)} fusion(bf16[1024,3072]{1,0:T(8,128)(2,1)} %copy-done.48, bf16[2048,3072]{1,0:T(8,128)(2,1)} %all-gather.6.cloned.1.call-done), kind=kOutput, calls=%fused_computation.225 | convolution fusion | flops 12884901888 | bytes 27262976 | tf_op jit(solution)/shard_map/dot_general | solution.py:46
  703.4 3.8 collective-permute-done.15
  712.8 4.1 all-to-all-start.3
  721.2 21.4 %all-to-all-done.3 = bf16[4,64,1024]{2,1,0:T(8,128)(2,1)} async-done(((bf16[4,64,1024]{2,1,0:T(8,128)(2,1)}), bf16[4,64,1024]{2,1,0:T(8,128)(2,1)}, u32[]{:S(2)}, u32[]{:S(2)}) %all-to-all-start.3) | async-done | bytes 524320 | tf_op jit(solution)/shard_map/all_to_all | solution.py:84
  748.2 2.7 fusion.24
  752.4 133.5 %reduce-scatter.8.cloned.1.call-done = bf16[256,3072]{1,0:T(8,128)(2,1)} async-done(((bf16[2048,3072]{1,0:T(8,128)(2,1)}), bf16[256,3072]{1,0:T(8,128)(2,1)}) %reduce-scatter.8.cloned.1.call-update) | async-done | bytes 1572880 | tf_op jit(solution)/shard_map/reduce_scatter | solution.py:92
  885.9 4.4 all-to-all-start.2
  890.2 4.0 fusion.72
  894.2 82.5 %reduce-scatter.10.cloned.1.call-done = bf16[128,2048]{1,0:T(8,128)(2,1)} async-done(((bf16[1024,2048]{1,0:T(8,128)(2,1)}), bf16[128,2048]{1,0:T(8,128)(2,1)}) %reduce-scatter.10.cloned.1.call-update) | async-done | bytes 524304 | tf_op jit(solution)/shard_map/reduce_scatter | solution.py:92
  978.4 3.3 add_convert_fusion.3
  981.7 132.5 %reduce-scatter.16.cloned.1.call-done = f32[64,4]{1,0:T(8,128)} async-done(((f32[2048,4]{1,0:T(8,128)}), f32[64,4]{1,0:T(8,128)}) %reduce-scatter.16.cloned.1.call-update) | async-done | bytes 1040
  (321 shorter events, 121.6 us)
Async XLA Ops:
  7.2 232.3 %all-gather.6.cloned.1.call-start = ((), (), s32[]{:S(2)}) async-start(), calls=%async_computation.9 | async-start | bytes 14155776 | tf_op jit(solution)/shard_map/all_gather | solution.py:88
  11.9 24.5 %copy-start.70 = (bf16[128,2048]{1,0:T(8,128)(2,1)S(1)}, bf16[128,2048]{1,0:T(8,128)(2,1)}, u32[]{:S(2)}) copy-start(bf16[128,2048]{1,0:T(8,128)(2,1)} %param.17) | copy-start | bytes 1572868
  12.0 26.0 %copy-start.64 = (bf16[64]{0:T(256)(128)(2,1)S(1)}, bf16[64]{0:T(256)(128)(2,1)}, u32[]{:S(2)}) copy-start(bf16[64]{0:T(256)(128)(2,1)} %param.19) | copy-start | bytes 388
  12.0 26.0 %copy-start.65 = (bf16[64]{0:T(256)(128)(2,1)S(1)}, bf16[64]{0:T(256)(128)(2,1)}, u32[]{:S(2)}) copy-start(bf16[64]{0:T(256)(128)(2,1)} %param.18) | copy-start | bytes 388
  12.0 26.0 %copy-start.66 = (bf16[64]{0:T(256)(128)(2,1)S(1)}, bf16[64]{0:T(256)(128)(2,1)}, u32[]{:S(2)}) copy-start(bf16[64]{0:T(256)(128)(2,1)} %param.15) | copy-start | bytes 388
  12.0 26.0 %copy-start.67 = (bf16[64]{0:T(256)(128)(2,1)S(1)}, bf16[64]{0:T(256)(128)(2,1)}, u32[]{:S(2)}) copy-start(bf16[64]{0:T(256)(128)(2,1)} %param.14) | copy-start | bytes 388
  12.0 132.2 %copy-start.4 = (bf16[256,2048]{1,0:T(8,128)(2,1)S(1)}, bf16[256,2048]{1,0:T(8,128)(2,1)}, u32[]{:S(2)}) copy-start(bf16[256,2048]{1,0:T(8,128)(2,1)} %param.11) | copy-start | bytes 3145732
  36.4 277.4 %all-gather.8.cloned.1.call-start = ((), (), s32[]{:S(2)}) async-start(), calls=%async_computation.10 | async-start | bytes 4718592 | tf_op jit(solution)/shard_map/all_gather | solution.py:88
  36.5 0.7 collective-permute-start.2
  145.4 3.7 copy-start.55
  146.9 10.4 copy-start.71
  146.9 26.2 %collective-permute-start = (bf16[1,256,2048]{2,1,0:T(8,128)(2,1)}, bf16[1,256,2048]{2,1,0:T(8,128)(2,1)S(1)}, u32[]{:S(2)}, u32[]{:S(2)}) collective-permute-start(bf16[1,256,2048]{2,1,0:T(8,128)(2,1)} %get-tuple-element.56), channel_id=1, source_target_pairs={{0,2},{1,3},{2,0},{3,1},{4,6},{5,7},{6,4},{7,5},{8,10},{9,11},{10,... | collective-permute-start | bytes 3145736 | tf_op jit(solution)/shard_map/ppermute | solution.py:55
  153.1 29.6 %all-to-all-start.1 = ((bf16[4,64,1024]{2,1,0:T(8,128)(2,1)}), bf16[4,64,1024]{2,1,0:T(8,128)(2,1)}, u32[]{:S(2)}, u32[]{:S(2)}) async-start(bf16[4,64,1024]{2,1,0:T(8,128)(2,1)} %reshape.737), calls=%async_computation.1 | async-start | bytes 1048576 | tf_op jit(solution)/shard_map/all_to_all | solution.py:84
  157.2 256.1 %all-gather.10.cloned.1.call-start = ((), (), s32[]{:S(2)}) async-start(), calls=%async_computation.11 | async-start | bytes 4718592 | tf_op jit(solution)/shard_map/all_gather | solution.py:88
  176.4 6.9 collective-permute-start.1
  178.4 114.1 %copy-start.61 = (f32[2]{0:T(128)}, f32[2]{0:T(128)S(1)}, u32[]{:S(2)}) copy-start(f32[2]{0:T(128)S(1)} %get-tuple-element.78) | copy-start | bytes 28
  178.5 113.1 %copy-start.59 = (f32[256,2]{0,1:T(2,128)}, f32[256,2]{0,1:T(2,128)S(1)}, u32[]{:S(2)}) copy-start(f32[256,2]{0,1:T(2,128)S(1)} %get-tuple-element.79) | copy-start | bytes 6148
  178.5 118.1 %copy-start.51 = (f32[256,2]{0,1:T(2,128)}, f32[256,2]{0,1:T(2,128)S(1)}, u32[]{:S(2)}) copy-start(f32[256,2]{0,1:T(2,128)S(1)} %get-tuple-element.80) | copy-start | bytes 6148
  179.5 117.2 %copy-start.72 = (bf16[4]{0:T(256)(128)(2,1)}, bf16[4]{0:T(256)(128)(2,1)S(1)}, u32[]{:S(2)}) copy-start(bf16[4]{0:T(256)(128)(2,1)S(1)} %pad.52.clone) | copy-start | bytes 28
  182.7 278.6 %all-gather.12.cloned.1.call-start = ((), (), s32[]{:S(2)}) async-start(), calls=%async_computation.12 | async-start | bytes 4718592 | tf_op jit(solution)/shard_map/all_gather | solution.py:88
  266.1 29.5 %copy-start.10 = (bf16[4,256,2,512]{3,2,1,0:T(2,128)(2,1)}, bf16[4,256,2,512]{3,2,1,0:T(2,128)(2,1)S(1)}, u32[]{:S(2)}) copy-start(bf16[4,256,2,512]{3,2,1,0:T(2,128)(2,1)S(1)} %reshape.733) | copy-start | bytes 6291460
  291.4 5.3 copy-start.23
  291.4 5.3 copy-start.25
  291.6 3.6 copy-start.16
  298.1 3.7 copy-start
  303.1 17.1 %copy-start.18 = (bf16[4,256,2,512]{1,3,2,0:T(8,128)(2,1)}, bf16[4,256,2,512]{1,3,2,0:T(8,128)(2,1)S(1)}, u32[]{:S(2)}) copy-start(bf16[4,256,2,512]{1,3,2,0:T(8,128)(2,1)S(1)} %multiply_convert_fusion.1) | copy-start | bytes 6291460
  320.2 4.0 copy-start.22
  324.2 4.4 collective-permute-start.3
  333.5 26.2 %collective-permute-start.4 = (bf16[1,256,2048]{2,1,0:T(8,128)(2,1)S(1)}, bf16[1,256,2048]{2,1,0:T(8,128)(2,1)}, u32[]{:S(2)}, u32[]{:S(2)}) collective-permute-start(bf16[1,256,2048]{2,1,0:T(8,128)(2,1)S(1)} %dynamic-slice_convert_fusion.4), channel_id=1, source_target_pairs={{0,2},{1,3},{2,0},{3,1},{4,6},{5,7},{6,4},{7,5},{8,10},{9,11},{10,... | collective-permute-start | bytes 3145736 | tf_op jit(solution)/shard_map/ppermute | solution.py:55
  335.1 377.7 %reduce-scatter.12.cloned.1.call-start = ((), (), s32[]{:S(2)}) async-start(), calls=%async_computation.15 | async-start | bytes 4718592 | tf_op jit(solution)/shard_map/reduce_scatter | solution.py:92
  335.1 46.9 %collective-permute-start.9 = (bf16[1,256,2048]{2,1,0:T(8,128)(2,1)}, bf16[1,256,2048]{2,1,0:T(8,128)(2,1)S(1)}, u32[]{:S(2)}, u32[]{:S(2)}) collective-permute-start(bf16[1,256,2048]{2,1,0:T(8,128)(2,1)} %bitcast.42), channel_id=1, source_target_pairs={{0,2},{1,3},{2,0},{3,1},{4,6},{5,7},{6,4},{7,5},{8,10},{9,11},{10,... | collective-permute-start | bytes 3145736 | tf_op jit(solution)/shard_map/ppermute | solution.py:55
  362.9 40.9 %collective-permute-start.5 = (bf16[1,256,2048]{2,1,0:T(8,128)(2,1)S(1)}, bf16[1,256,2048]{2,1,0:T(8,128)(2,1)S(1)}, u32[]{:S(2)}, u32[]{:S(2)}) collective-permute-start(bf16[1,256,2048]{2,1,0:T(8,128)(2,1)S(1)} %fusion.126), channel_id=1, source_target_pairs={{0,2},{1,3},{2,0},{3,1},{4,6},{5,7},{6,4},{7,5},{8,10},{9,11},{10,... | collective-permute-start | bytes 3145736 | tf_op jit(solution)/shard_map/ppermute | solution.py:55
  384.0 22.1 %collective-permute-start.10 = (bf16[2,256,2048]{2,1,0:T(8,128)(2,1)S(1)}, bf16[2,256,2048]{2,1,0:T(8,128)(2,1)S(1)}, u32[]{:S(2)}, u32[]{:S(2)}) collective-permute-start(bf16[2,256,2048]{2,1,0:T(8,128)(2,1)S(1)} %maximum_select_fusion.8), channel_id=1, source_target_pairs={{0,1},{1,0},{2,3},{3,2},{4,5},{5,4},{6,7},{7,6},{8,9},{9,8},{10,11... | collective-permute-start | bytes 6291464 | tf_op jit(solution)/shard_map/ppermute | solution.py:55
  404.1 6.2 collective-permute-start.6
  461.3 16.9 %copy-start.34 = (f32[1024,1024]{1,0:T(8,128)S(1)}, f32[1024,1024]{1,0:T(8,128)}, u32[]{:S(2)}) copy-start(f32[1024,1024]{1,0:T(8,128)} %fusion.86) | copy-start | bytes 12582916
  478.2 3.7 copy-start.33
  488.1 230.9 %reduce-scatter.14.cloned.1.call-start = ((), (), s32[]{:S(2)}) async-start(), calls=%async_computation.16 | async-start | bytes 4718592 | tf_op jit(solution)/shard_map/reduce_scatter | solution.py:92
  488.2 7.8 copy-start.69
  495.9 6.2 collective-permute-start.11
  502.0 4.4 collective-permute-start.7
  503.0 48.3 %copy-start.9 = (f32[2,256,2048]{2,1,0:T(8,128)}, f32[2,256,2048]{2,1,0:T(8,128)S(1)}, u32[]{:S(2)}) copy-start(f32[2,256,2048]{2,1,0:T(8,128)S(1)} %bitcast_add_fusion.1) | copy-start | bytes 12582916
  503.1 26.0 %collective-permute-start.12 = (bf16[1,256,2048]{2,1,0:T(8,128)(2,1)S(1)}, bf16[1,256,2048]{2,1,0:T(8,128)(2,1)S(1)}, u32[]{:S(2)}, u32[]{:S(2)}) collective-permute-start(bf16[1,256,2048]{2,1,0:T(8,128)(2,1)S(1)} %dynamic-slice_convert_fusion.2), channel_id=1, source_target_pairs={{0,2},{1,3},{2,0},{3,1},{4,6},{5,7},{6,4},{7,5},{8,10},{9,11},{10,... | collective-permute-start | bytes 3145736 | tf_op jit(solution)/shard_map/ppermute | solution.py:55
  509.0 42.2 %collective-permute-start.8 = (bf16[1,256,2048]{2,1,0:T(8,128)(2,1)S(1)}, bf16[1,256,2048]{2,1,0:T(8,128)(2,1)S(1)}, u32[]{:S(2)}, u32[]{:S(2)}) collective-permute-start(bf16[1,256,2048]{2,1,0:T(8,128)(2,1)S(1)} %dynamic-slice_convert_fusion.3), channel_id=1, source_target_pairs={{0,2},{1,3},{2,0},{3,1},{4,6},{5,7},{6,4},{7,5},{8,10},{9,11},{10,... | collective-permute-start | bytes 3145736 | tf_op jit(solution)/shard_map/ppermute | solution.py:55
  529.1 22.1 %copy-start.14 = (bf16[1,256,2048]{2,1,0:T(8,128)(2,1)}, bf16[1,256,2048]{2,1,0:T(8,128)(2,1)S(1)}, u32[]{:S(2)}) copy-start(bf16[1,256,2048]{2,1,0:T(8,128)(2,1)S(1)} %collective-permute-done.12) | copy-start | bytes 3145732
  555.5 26.5 %copy-start.32 = (bf16[2,2,256,2048]{3,2,1,0:T(8,128)(2,1)S(1)}, bf16[2,2,256,2048]{3,2,1,0:T(8,128)(2,1)}, u32[]{:S(2)}) copy-start(bf16[2,2,256,2048]{3,2,1,0:T(8,128)(2,1)} %copy.213) | copy-start | bytes 12582916
  555.5 24.8 %collective-permute-start.13 = (bf16[1,256,2048]{2,1,0:T(8,128)(2,1)S(1)}, bf16[1,256,2048]{2,1,0:T(8,128)(2,1)S(1)}, u32[]{:S(2)}, u32[]{:S(2)}) collective-permute-start(bf16[1,256,2048]{2,1,0:T(8,128)(2,1)S(1)} %fusion.124), channel_id=1, source_target_pairs={{0,2},{1,3},{2,0},{3,1},{4,6},{5,7},{6,4},{7,5},{8,10},{9,11},{10,... | collective-permute-start | bytes 3145736 | tf_op jit(solution)/shard_map/ppermute | solution.py:55
  582.0 10.0 collective-permute-start.14
  588.5 297.4 %reduce-scatter.8.cloned.1.call-start = ((), (), s32[]{:S(2)}) async-start(), calls=%async_computation.13 | async-start | bytes 14155776 | tf_op jit(solution)/shard_map/reduce_scatter | solution.py:92
  592.0 3.8 copy-start.68
  595.0 3.8 copy-start.1
  595.0 5.1 copy-start.3
  595.6 9.8 copy-start.30
  616.5 3.7 copy-start.12
  648.7 4.5 copy-start.29
  648.8 3.2 copy-start.48
  669.1 307.6 %reduce-scatter.10.cloned.1.call-start = ((), (), s32[]{:S(2)}) async-start(), calls=%async_computation.14 | async-start | bytes 4718592 | tf_op jit(solution)/shard_map/reduce_scatter | solution.py:92
  702.7 4.4 collective-permute-start.15
  710.1 7.0 copy-start.15
  711.3 34.6 %collective-permute-start.16 = (bf16[1,256,2048]{2,1,0:T(8,128)(2,1)}, bf16[1,256,2048]{2,1,0:T(8,128)(2,1)}, u32[]{:S(2)}, u32[]{:S(2)}) collective-permute-start(bf16[1,256,2048]{2,1,0:T(8,128)(2,1)} %dynamic-slice_convert_fusion.1), channel_id=1, source_target_pairs={{0,2},{1,3},{2,0},{3,1},{4,6},{5,7},{6,4},{7,5},{8,10},{9,11},{10,... | collective-permute-start | bytes 3145736 | tf_op jit(solution)/shard_map/ppermute | solution.py:55
  712.8 29.9 %all-to-all-start.3 = ((bf16[4,64,1024]{2,1,0:T(8,128)(2,1)}), bf16[4,64,1024]{2,1,0:T(8,128)(2,1)}, u32[]{:S(2)}, u32[]{:S(2)}) async-start(bf16[4,64,1024]{2,1,0:T(8,128)(2,1)} %bitcast.289), calls=%async_computation.6 | async-start | bytes 1048576 | tf_op jit(solution)/shard_map/all_to_all | solution.py:84
  716.9 397.3 %reduce-scatter.16.cloned.1.call-start = ((), (), s32[]{:S(2)}) async-start(), calls=%async_computation.17 | async-start | bytes 1081344
  748.2 4.1 copy-start.58
  885.9 232.7 %all-to-all-start.2 = ((bf16[4,64,3072]{2,1,0:T(8,128)(2,1)}), bf16[4,64,3072]{2,1,0:T(8,128)(2,1)}, u32[]{:S(2)}, u32[]{:S(2)}) async-start(bf16[4,64,3072]{2,1,0:T(8,128)(2,1)} %bitcast.286), calls=%async_computation.3 | async-start | bytes 3145728 | tf_op jit(solution)/shard_map/all_to_all | solution.py:84
  976.7 140.8 %collective-permute-start.17 = (bf16[128,2048]{1,0:T(8,128)(2,1)}, bf16[128,2048]{1,0:T(8,128)(2,1)S(1)}, u32[]{:S(2)}, u32[]{:S(2)}) collective-permute-start(bf16[128,2048]{1,0:T(8,128)(2,1)} %reduce-scatter.10.cloned.1.call-done), channel_id=1, source_target_pairs={{0,0},{4,1},{8,2},{12,3},{16,4},{20,5},{24,6},{28,7},{1,8},{5,9},{... | collective-permute-start | bytes 1572872 | tf_op jit(solution)/shard_map/ppermute | solution.py:207
  (41 other events, 71.2 us)
Sparse Core Ops, SparseCore 0:
  36.5 202.9 all-gather.5
  242.2 71.5 all-gather.7
  315.9 71.6 all-gather.9
  389.6 71.6 all-gather.11
  488.3 86.3 reduce-scatter.11
  588.6 86.5 reduce-scatter.13
  678.8 206.9 reduce-scatter.7
  889.5 87.1 reduce-scatter.9
  979.6 134.5 reduce-scatter.15
where the time goes:
time: 1140 us; the launch traced here: 1130 us
  waiting for transfers between devices  620 us (54%)
  matrix products  131 us (11%)
  blocking collectives  130 us (11%)
  local copies, waits for them, and re-layouts  127 us (11%)
  other arithmetic  78 us (7%)
  starting transfers between devices  26.5 us (2%)
  between operations  16.3 us (1%)
    reduce_scatter x4, waiting for transfers between devices, scatter_dp(): lax.psum_scatter(x.astype(bf16), 'dp', scatter_dimension=0, tiled=True)  216 us
    ppermute x16, waiting for transfers between devices, swap_seq(): return lax.ppermute(x, 'seq', [(i, i ^ bit) for i in range(size)])  150 us
    unnamed x10, waiting for transfers between devices  133 us
    dot_general x12, matrix products, dot(): return lax.dot_general(a, b, (dims, ((), ())), preferred_element_type=f32)  120 us
    all_gather x1, blocking collectives, local(): lax.all_gather(jnp.stack([norm1_gain, norm1_shift, norm2_gain, norm2_shif...  106 us
    all_gather x4, waiting for transfers between devices, gather_dp(): return lax.all_gather(x, 'dp', axis=0, tiled=True)  99.8 us
    unnamed x166, local copies, waits for them, and re-layouts  45.7 us
    all_to_all x1, blocking collectives, exchange_seq(): return lax.all_to_all(x, 'seq', 0, 0)  24.4 us
  transfers between devices with their start and end apart: 30, of which 17 were waited for; matrix products, arithmetic and copies ran while one was open for 24% of the time, Pallas kernels for 0%

commit v1 on v0

--- a/solution.py
+++ b/solution.py
@@ -85,7 +85,31 @@
 
 
 def gather_dp(x):
-    return lax.all_gather(x, "dp", axis=0, tiled=True)
+
+    def _meet_core(arr, group_axis):
+        next_value = lax.axis_size(group_axis)
+        response, passed, r2 = (next_value, lax.axis_index(group_axis), arr.shape[0])
+        items = [i0 * response if nth == 0 else i0 for nth, i0 in enumerate(arr.shape)]
+        oldest = jnp.zeros(items, arr.dtype)
+        carry_in = lax.dynamic_update_slice_in_dim(oldest, arr, passed * r2, axis=0)
+        found_now = opened = arr
+        for idx in range(1, response // 2 + 1):
+            found_now = lax.ppermute(
+                found_now, group_axis, [(nth, (nth + 1) % response) for nth in range(response)]
+            )
+            carry_in = lax.dynamic_update_slice_in_dim(
+                carry_in, found_now, (passed - idx) % response * r2, axis=0
+            )
+            if 2 * idx < response:
+                opened = lax.ppermute(
+                    opened, group_axis, [(nth, (nth - 1) % response) for nth in range(response)]
+                )
+                carry_in = lax.dynamic_update_slice_in_dim(
+                    carry_in, opened, (passed + idx) % response * r2, axis=0
+                )
+        return carry_in
+
+    return _meet_core(x, "dp")
 
 
 def scatter_dp(x):

time: 1140 us -> 1380 us (1.21)
  waiting for transfers between devices: 620 us -> 806 us
  starting transfers between devices: 26.5 us -> 75.7 us
  local copies, waits for them, and re-layouts: 127 us -> 171 us
  blocking collectives: 130 us -> 86.5 us
    ppermute x0 -> x28, waiting for transfers between devices: none -> 360 us  [the longest x12 236 us: _meet_core(): lax.ppermute(opened, group_axis, [(nth, (nth - 1) % response) for nth in...]
    all_gather x4 -> x0, waiting for transfers between devices: 99.8 us -> none  [gather_dp(): return lax.all_gather(x, 'dp', axis=0, tiled=True)]
    ppermute x16, waiting for transfers between devices: 150 us -> 76.7 us  [swap_seq(): return lax.ppermute(x, 'seq', [(i, i ^ bit) for i in range(size)])]
    ppermute x0 -> x28, starting transfers between devices: none -> 48.5 us  [the longest x12 36.8 us: _meet_core(): lax.ppermute(opened, group_axis, [(nth, (nth - 1) % response) for nth in...]
    all_gather x1, blocking collectives: 106 us -> 57.7 us  [local(): lax.all_gather(jnp.stack([norm1_gain, norm1_shift, norm2_gain, norm2_shif...]
    dynamic_update_slice x0 -> x31, local copies, waits for them, and re-layouts: none -> 33.1 us  [the longest x15 18.9 us: _meet_core(): lax.dynamic_update_slice_in_dim(carry_in, found_now, (passed - idx) % res...]
    unnamed x166 -> x188, local copies, waits for them, and re-layouts: 45.7 us -> 44.7 us
    unnamed x10 -> x6, waiting for transfers between devices: 133 us -> 132 us
  transfers between devices with their start and end apart: 30 -> 54, of which waited for: 17 -> 27; matrix products, arithmetic and copies ran while one was open for 24% -> 17% of each run, Pallas kernels for 0% -> 0%
where the time goes in v1:
time: 1380 us; the launch traced here: 1370 us
  waiting for transfers between devices  806 us (58%)
  local copies, waits for them, and re-layouts  171 us (12%)
  matrix products  133 us (10%)
  blocking collectives  86.5 us (6%)
  other arithmetic  78.7 us (6%)
  starting transfers between devices  75.7 us (5%)
  between operations  17 us (1%)
    ppermute x12, waiting for transfers between devices, _meet_core(): lax.ppermute(opened, group_axis, [(nth, (nth - 1) % response) for nth in...  236 us
    reduce_scatter x4, waiting for transfers between devices, scatter_dp(): lax.psum_scatter(x.astype(bf16), 'dp', scatter_dimension=0, tiled=True)  214 us
    unnamed x6, waiting for transfers between devices  132 us
    ppermute x16, waiting for transfers between devices, _meet_core(): lax.ppermute(found_now, group_axis, [(nth, (nth + 1) % response) for nth...  124 us
    dot_general x12, matrix products, dot(): return lax.dot_general(a, b, (dims, ((), ())), preferred_element_type=f32)  122 us
    ppermute x16, waiting for transfers between devices, swap_seq(): return lax.ppermute(x, 'seq', [(i, i ^ bit) for i in range(size)])  76.7 us
    all_gather x1, blocking collectives, local(): lax.all_gather(jnp.stack([norm1_gain, norm1_shift, norm2_gain, norm2_shif...  57.7 us
    unnamed x188, local copies, waits for them, and re-layouts  44.7 us
  transfers between devices with their start and end apart: 54, of which 27 were waited for; matrix products, arithmetic and copies ran while one was open for 17% of the time, Pallas kernels for 0%

profile of v1, /device:TPU:0, one launch (start us, length us, event | category | flops | bytes accessed | tf_op | source)
XLA Modules:
  0.0 1368.1 jit_solution(7161195568212895980)
XLA Ops:
  7.2 6.0 collective-permute-start.29
  13.2 5.4 collective-permute-start.9
  28.9 57.7 %all-gather = bf16[32,64,4]{1,2,0:T(4,128)(2,1)S(1)} all-gather(bf16[1,64,4]{1,2,0:T(4,128)(2,1)S(1)} %maximum_bitcast_fusion.1), channel_id=1, replica_groups=mesh['dp'=8,'seq'=4] {'dp','seq'}, dimensions={0}, use_global_device_ids=true | all-gather | bytes 16896 | tf_op jit(solution)/shard_map/all_gather | solution.py:140
  98.5 4.5 collective-permute-start.11
  107.4 4.7 collective-permute-start.31
  117.8 4.0 maximum_select_fusion.4
  121.7 47.9 %collective-permute-done.11 = bf16[128,2048]{1,0:T(8,128)(2,1)S(1)} collective-permute-done((bf16[128,2048]{1,0:T(8,128)(2,1)}, bf16[128,2048]{1,0:T(8,128)(2,1)S(1)}, u32[]{:S(2)}, u32[]{:S(2)}) %collective-permute-start.11) | collective-permute-done | bytes 524320 | tf_op jit(solution)/shard_map/ppermute | solution.py:104
  174.8 39.8 %collective-permute-done.31 = bf16[128,2048]{1,0:T(8,128)(2,1)S(1)} collective-permute-done((bf16[128,2048]{1,0:T(8,128)(2,1)}, bf16[128,2048]{1,0:T(8,128)(2,1)S(1)}, u32[]{:S(2)}, u32[]{:S(2)}) %collective-permute-start.31) | collective-permute-done | bytes 524320 | tf_op jit(solution)/shard_map/ppermute | solution.py:104
  214.6 7.7 collective-permute-done.30
  222.3 3.9 collective-permute-start.33
  228.9 8.1 collective-permute-done.13
  237.1 6.2 broadcast_in_dim.45
  244.5 34.0 %collective-permute-done.12 = bf16[128,2048]{1,0:T(8,128)(2,1)} collective-permute-done((bf16[128,2048]{1,0:T(8,128)(2,1)}, bf16[128,2048]{1,0:T(8,128)(2,1)}, u32[]{:S(2)}, u32[]{:S(2)}) %collective-permute-start.12) | collective-permute-done | bytes 524320 | tf_op jit(solution)/shard_map/ppermute | solution.py:97
  278.5 3.9 collective-permute-start.15
  282.4 10.8 collective-permute-done.33
  295.3 5.6 collective-permute-done.32
  301.8 3.9 collective-permute-start.5
  307.6 8.1 collective-permute-done.15
  315.7 30.1 %collective-permute-done.14 = bf16[128,2048]{1,0:T(8,128)(2,1)S(1)} collective-permute-done((bf16[128,2048]{1,0:T(8,128)(2,1)}, bf16[128,2048]{1,0:T(8,128)(2,1)S(1)}, u32[]{:S(2)}, u32[]{:S(2)}) %collective-permute-start.14) | collective-permute-done | bytes 524320 | tf_op jit(solution)/shard_map/ppermute | solution.py:97
  351.8 5.3 collective-permute-done.34
  357.1 11.1 collective-permute-done.16
  372.0 33.1 %collective-permute-done.5 = bf16[256,3072]{1,0:T(8,128)(2,1)S(1)} collective-permute-done((bf16[256,3072]{1,0:T(8,128)(2,1)}, bf16[256,3072]{1,0:T(8,128)(2,1)S(1)}, u32[]{:S(2)}, u32[]{:S(2)}) %collective-permute-start.5) | collective-permute-done | bytes 1572896 | tf_op jit(solution)/shard_map/ppermute | solution.py:104
  417.6 56.9 %collective-permute-done.7 = bf16[256,3072]{1,0:T(8,128)(2,1)S(1)} collective-permute-done((bf16[256,3072]{1,0:T(8,128)(2,1)S(1)}, bf16[256,3072]{1,0:T(8,128)(2,1)S(1)}, u32[]{:S(2)}, u32[]{:S(2)}) %collective-permute-start.7) | collective-permute-done | bytes 1572896 | tf_op jit(solution)/shard_map/ppermute | solution.py:104
  476.3 15.6 %fusion.85 = f32[1024,3072]{1,0:T(8,128)} fusion(bf16[1024,2048]{1,0:T(8,128)(2,1)S(1)} %bitcast.268, bf16[2048,3072]{1,0:T(8,128)(2,1)S(1)} %constant_dynamic-update-slice_fusion.24), kind=kOutput, calls=%fused_computation.252 | convolution fusion | flops 12884901888 | bytes 29360128 | tf_op jit(solution)/shard_map/dot_general | solution.py:46
  491.9 3.8 slice.229
  495.7 4.8 slice.144
  500.6 4.7 fusion.77
  508.6 4.3 reshape.734
  512.8 6.6 reshape.732
  519.4 7.3 copy.200
  526.7 3.9 reshape.735
  545.6 7.2 fusion.8
  556.1 4.3 collective-permute-done.17
  568.1 28.7 %all_to_all.20 = bf16[4,64,1024]{2,1,0:T(8,128)(2,1)S(1)} all-to-all(bf16[4,64,1024]{2,1,0:T(8,128)(2,1)S(1)} %reshape.737), channel_id=1, replica_groups=mesh['dp'=8,'seq'=4] {'seq'}, dimensions={0} | all-to-all | bytes 1048576 | tf_op jit(solution)/shard_map/all_to_all | solution.py:84
  598.7 4.3 collective-permute-start.22
  603.0 16.4 %collective-permute-done.21 = bf16[256,1024]{1,0:T(8,128)(2,1)S(1)} collective-permute-done((bf16[256,1024]{1,0:T(8,128)(2,1)S(1)}, bf16[256,1024]{1,0:T(8,128)(2,1)S(1)}, u32[]{:S(2)}, u32[]{:S(2)}) %collective-permute-start.21) | collective-permute-done | bytes 524320 | tf_op jit(solution)/shard_map/ppermute | solution.py:97
  631.1 13.6 collective-permute-done.23
  647.9 10.5 collective-permute-done.24
  662.8 20.6 %collective-permute-done.26 = bf16[256,1024]{1,0:T(8,128)(2,1)S(1)} collective-permute-done((bf16[256,1024]{1,0:T(8,128)(2,1)S(1)}, bf16[256,1024]{1,0:T(8,128)(2,1)S(1)}, u32[]{:S(2)}, u32[]{:S(2)}) %collective-permute-start.26) | collective-permute-done | bytes 524320 | tf_op jit(solution)/shard_map/ppermute | solution.py:104
  687.0 4.5 fusion.86
  691.5 16.8 %add_convert_fusion.2 = (bf16[1024,1024]{1,0:T(8,128)(2,1)S(1)}, f32[1024,1024]{1,0:T(8,128)}) fusion(f32[1024,1024]{1,0:T(8,128)S(1)} %fusion.86, bf16[1024,2048]{1,0:T(8,128)(2,1)S(1)} %bitcast.272, bf16[1024,2048]{1,0:T(8,128)(2,1)} %get-tuple-element.89), kind=kOutput, calls=%fused_computation.31 | convolution fusion | flops 4370464768 | bytes 18874368 | tf_op jit(solution)/shard_map/dot_general | solution.py:46
  709.7 6.6 convolution_convert_fusion.2
  716.3 10.8 fusion.88
  732.4 6.8 fusion.87
  745.7 22.8 %collective-permute-done.40 = bf16[1,256,2048]{2,1,0:T(8,128)(2,1)S(1)} collective-permute-done((bf16[1,256,2048]{2,1,0:T(8,128)(2,1)S(1)}, bf16[1,256,2048]{2,1,0:T(8,128)(2,1)S(1)}, u32[]{:S(2)}, u32[]{:S(2)}) %collective-permute-start.40) | collective-permute-done | bytes 1048608 | tf_op jit(solution)/shard_map/ppermute | solution.py:55
  769.3 21.1 %collective-permute-done.36 = bf16[1,256,2048]{2,1,0:T(8,128)(2,1)S(1)} collective-permute-done((bf16[1,256,2048]{2,1,0:T(8,128)(2,1)S(1)}, bf16[1,256,2048]{2,1,0:T(8,128)(2,1)S(1)}, u32[]{:S(2)}, u32[]{:S(2)}) %collective-permute-start.36) | collective-permute-done | bytes 1048608 | tf_op jit(solution)/shard_map/ppermute | solution.py:55
  795.4 24.0 %collective-permute-done.41 = bf16[1,256,2048]{2,1,0:T(8,128)(2,1)S(1)} collective-permute-done((bf16[1,256,2048]{2,1,0:T(8,128)(2,1)S(1)}, bf16[1,256,2048]{2,1,0:T(8,128)(2,1)S(1)}, u32[]{:S(2)}, u32[]{:S(2)}) %collective-permute-start.41) | collective-permute-done | bytes 1048608 | tf_op jit(solution)/shard_map/ppermute | solution.py:55
  821.2 6.3 convolution_convert_fusion.1
  839.2 7.3 multiply_reduce_fusion
  846.5 4.6 fusion.73
  851.1 6.1 copy.235
  877.9 6.3 copy.232
  890.9 15.9 %convolution_convert_fusion = bf16[2048,3072]{1,0:T(8,128)(2,1)} fusion(bf16[1024,2048]{1,0:T(8,128)(2,1)S(1)} %bitcast.269, bf16[1024,3072]{1,0:T(8,128)(2,1)S(1)} %constant_dynamic-update-slice_fusion.32), kind=kOutput, calls=%fused_computation | convolution fusion | flops 12891193344 | bytes 23068672 | tf_op jit(solution)/shard_map/dot_general | solution.py:46
  906.9 6.2 copy.241
  915.9 6.3 convolution_convert_fusion.3
  922.3 17.9 %fusion.90 = f32[1024,2048]{1,0:T(8,128)S(1)} fusion(bf16[1024,3072]{1,0:T(8,128)(2,1)} %copy-done.58, bf16[2048,3072]{1,0:T(8,128)(2,1)} %copy-done.15), kind=kOutput, calls=%fused_computation.257 | convolution fusion | flops 12884901888 | bytes 27262976 | tf_op jit(solution)/shard_map/dot_general | solution.py:46
  941.1 3.8 collective-permute-done.43
  948.9 4.1 all-to-all-start.3
  957.4 22.8 %all-to-all-done.3 = bf16[4,64,1024]{2,1,0:T(8,128)(2,1)} async-done(((bf16[4,64,1024]{2,1,0:T(8,128)(2,1)}), bf16[4,64,1024]{2,1,0:T(8,128)(2,1)}, u32[]{:S(2)}, u32[]{:S(2)}) %all-to-all-start.3) | async-done | bytes 524320 | tf_op jit(solution)/shard_map/all_to_all | solution.py:84
  992.2 132.1 %reduce-scatter.8.cloned.1.call-done = bf16[256,3072]{1,0:T(8,128)(2,1)} async-done(((bf16[2048,3072]{1,0:T(8,128)(2,1)}), bf16[256,3072]{1,0:T(8,128)(2,1)}) %reduce-scatter.8.cloned.1.call-update) | async-done | bytes 1572880 | tf_op jit(solution)/shard_map/reduce_scatter | solution.py:116
  1124.3 4.3 all-to-all-start.2
  1128.6 4.0 fusion.72
  1132.6 82.4 %reduce-scatter.10.cloned.1.call-done = bf16[128,2048]{1,0:T(8,128)(2,1)} async-done(((bf16[1024,2048]{1,0:T(8,128)(2,1)}), bf16[128,2048]{1,0:T(8,128)(2,1)}) %reduce-scatter.10.cloned.1.call-update) | async-done | bytes 524304 | tf_op jit(solution)/shard_map/reduce_scatter | solution.py:116
  1219.9 132.4 %reduce-scatter.16.cloned.1.call-done = f32[64,4]{1,0:T(8,128)} async-done(((f32[2048,4]{1,0:T(8,128)}), f32[64,4]{1,0:T(8,128)}) %reduce-scatter.16.cloned.1.call-update) | async-done | bytes 1040
  (423 shorter events, 219.6 us)
Async XLA Ops:
  7.2 100.2 %collective-permute-start.29 = (bf16[128,2048]{1,0:T(8,128)(2,1)}, bf16[128,2048]{1,0:T(8,128)(2,1)}, u32[]{:S(2)}, u32[]{:S(2)}) collective-permute-start(bf16[128,2048]{1,0:T(8,128)(2,1)} %param.21), channel_id=1, source_target_pairs={{0,28},{4,0},{8,4},{12,8},{16,12},{20,16},{24,20},{28,24},{1,29},{... | collective-permute-start | bytes 1572872 | tf_op jit(solution)/shard_map/ppermute | solution.py:104
  13.2 94.2 %collective-permute-start.28 = (bf16[128,2048]{1,0:T(8,128)(2,1)}, bf16[128,2048]{1,0:T(8,128)(2,1)}, u32[]{:S(2)}, u32[]{:S(2)}) collective-permute-start(bf16[128,2048]{1,0:T(8,128)(2,1)} %param.21), channel_id=1, source_target_pairs={{0,4},{4,8},{8,12},{12,16},{16,20},{20,24},{24,28},{28,0},{1,5},{5... | collective-permute-start | bytes 1572872 | tf_op jit(solution)/shard_map/ppermute | solution.py:97
  13.2 85.3 %collective-permute-start.9 = (bf16[128,2048]{1,0:T(8,128)(2,1)}, bf16[128,2048]{1,0:T(8,128)(2,1)}, u32[]{:S(2)}, u32[]{:S(2)}) collective-permute-start(bf16[128,2048]{1,0:T(8,128)(2,1)} %param.17), channel_id=1, source_target_pairs={{0,0},{1,4},{2,8},{3,12},{4,16},{5,20},{6,24},{7,28},{8,1},{9,5},{... | collective-permute-start | bytes 1572872 | tf_op jit(solution)/shard_map/ppermute | solution.py:154
  24.5 73.6 %all-to-all-start = ((bf16[4,64,3072]{2,1,0:T(8,128)(2,1)}), bf16[4,64,3072]{2,1,0:T(8,128)(2,1)S(1)}, u32[]{:S(2)}, u32[]{:S(2)}) async-start(bf16[4,64,3072]{2,1,0:T(8,128)(2,1)} %copy.198), calls=%async_computation | async-start | bytes 3145728 | tf_op jit(solution)/shard_map/all_to_all | solution.py:84
  28.1 920.8 %reduce-scatter.12.cloned.1.call-start = ((), (), s32[]{:S(2)}) async-start(), calls=%async_computation.11 | async-start | bytes 4718592 | tf_op jit(solution)/shard_map/reduce_scatter | solution.py:116
  28.3 60.3 %copy-start.65 = (f32[256]{0:T(256)}, f32[256]{0:T(256)S(1)}, u32[]{:S(2)}) copy-start(f32[256]{0:T(256)S(1)} %broadcast_multiply_fusion.2) | copy-start | bytes 3076
  28.8 58.0 %copy-start.69 = (f32[256]{0:T(256)}, f32[256]{0:T(256)S(1)}, u32[]{:S(2)}) copy-start(f32[256]{0:T(256)S(1)} %fusion.25) | copy-start | bytes 3076
  28.8 63.2 %copy-start.56 = (bf16[128,2048]{1,0:T(8,128)(2,1)S(1)}, bf16[128,2048]{1,0:T(8,128)(2,1)}, u32[]{:S(2)}) copy-start(bf16[128,2048]{1,0:T(8,128)(2,1)} %param.21) | copy-start | bytes 1572868
  28.8 59.8 %copy-start.67 = (f32[256]{0:T(256)}, f32[256]{0:T(256)S(1)}, u32[]{:S(2)}) copy-start(f32[256]{0:T(256)S(1)} %fusion.62) | copy-start | bytes 3076
  88.6 27.3 %collective-permute-start = (bf16[1,256,2048]{2,1,0:T(8,128)(2,1)}, bf16[1,256,2048]{2,1,0:T(8,128)(2,1)}, u32[]{:S(2)}, u32[]{:S(2)}) collective-permute-start(bf16[1,256,2048]{2,1,0:T(8,128)(2,1)} %get-tuple-element.56), channel_id=1, source_target_pairs={{0,2},{1,3},{2,0},{3,1},{4,6},{5,7},{6,4},{7,5},{8,10},{9,11},{10,... | collective-permute-start | bytes 3145736 | tf_op jit(solution)/shard_map/ppermute | solution.py:55
  89.5 446.2 %copy-start.71 = (f32[256,2]{0,1:T(2,128)}, f32[256,2]{0,1:T(2,128)S(1)}, u32[]{:S(2)}) copy-start(f32[256,2]{0,1:T(2,128)S(1)} %get-tuple-element.79) | copy-start | bytes 6148
  89.5 449.7 %copy-start.63 = (f32[256,2]{0,1:T(2,128)}, f32[256,2]{0,1:T(2,128)S(1)}, u32[]{:S(2)}) copy-start(f32[256,2]{0,1:T(2,128)S(1)} %get-tuple-element.80) | copy-start | bytes 6148
  98.1 75.8 %collective-permute-start.2 = (bf16[256,3072]{1,0:T(8,128)(2,1)S(1)}, bf16[256,3072]{1,0:T(8,128)(2,1)}, u32[]{:S(2)}, u32[]{:S(2)}) collective-permute-start(bf16[256,3072]{1,0:T(8,128)(2,1)S(1)} %bitcast.254), channel_id=1, source_target_pairs={{0,4},{4,8},{8,12},{12,16},{16,20},{20,24},{24,28},{28,0},{1,5},{5... | collective-permute-start | bytes 4718600 | tf_op jit(solution)/shard_map/ppermute | solution.py:97
  98.2 438.4 %copy-start.73 = (f32[2]{0:T(128)}, f32[2]{0:T(128)S(1)}, u32[]{:S(2)}) copy-start(f32[2]{0:T(128)S(1)} %get-tuple-element.78) | copy-start | bytes 28
  98.5 440.7 %copy-start.81 = (bf16[4]{0:T(256)(128)(2,1)}, bf16[4]{0:T(256)(128)(2,1)S(1)}, u32[]{:S(2)}) copy-start(bf16[4]{0:T(256)(128)(2,1)S(1)} %pad.52.clone) | copy-start | bytes 28
  98.5 71.2 %collective-permute-start.11 = (bf16[128,2048]{1,0:T(8,128)(2,1)}, bf16[128,2048]{1,0:T(8,128)(2,1)S(1)}, u32[]{:S(2)}, u32[]{:S(2)}) collective-permute-start(bf16[128,2048]{1,0:T(8,128)(2,1)} %collective-permute-done.9), channel_id=1, source_target_pairs={{0,28},{4,0},{8,4},{12,8},{16,12},{20,16},{24,20},{28,24},{1,29},{... | collective-permute-start | bytes 1572872 | tf_op jit(solution)/shard_map/ppermute | solution.py:104
  107.4 62.3 %collective-permute-start.10 = (bf16[128,2048]{1,0:T(8,128)(2,1)}, bf16[128,2048]{1,0:T(8,128)(2,1)}, u32[]{:S(2)}, u32[]{:S(2)}) collective-permute-start(bf16[128,2048]{1,0:T(8,128)(2,1)} %collective-permute-done.9), channel_id=1, source_target_pairs={{0,4},{4,8},{8,12},{12,16},{16,20},{20,24},{24,28},{28,0},{1,5},{5... | collective-permute-start | bytes 1572872 | tf_op jit(solution)/shard_map/ppermute | solution.py:97
  107.4 107.2 %collective-permute-start.31 = (bf16[128,2048]{1,0:T(8,128)(2,1)}, bf16[128,2048]{1,0:T(8,128)(2,1)S(1)}, u32[]{:S(2)}, u32[]{:S(2)}) collective-permute-start(bf16[128,2048]{1,0:T(8,128)(2,1)} %collective-permute-done.29), channel_id=1, source_target_pairs={{0,28},{4,0},{8,4},{12,8},{16,12},{20,16},{24,20},{28,24},{1,29},{... | collective-permute-start | bytes 1572872 | tf_op jit(solution)/shard_map/ppermute | solution.py:104
  115.8 106.4 %collective-permute-start.30 = (bf16[128,2048]{1,0:T(8,128)(2,1)}, bf16[128,2048]{1,0:T(8,128)(2,1)}, u32[]{:S(2)}, u32[]{:S(2)}) collective-permute-start(bf16[128,2048]{1,0:T(8,128)(2,1)} %collective-permute-done.28), channel_id=1, source_target_pairs={{0,4},{4,8},{8,12},{12,16},{16,20},{20,24},{24,28},{28,0},{1,5},{5... | collective-permute-start | bytes 1572872 | tf_op jit(solution)/shard_map/ppermute | solution.py:97
  169.7 67.4 %collective-permute-start.13 = (bf16[128,2048]{1,0:T(8,128)(2,1)S(1)}, bf16[128,2048]{1,0:T(8,128)(2,1)S(1)}, u32[]{:S(2)}, u32[]{:S(2)}) collective-permute-start(bf16[128,2048]{1,0:T(8,128)(2,1)S(1)} %collective-permute-done.11), channel_id=1, source_target_pairs={{0,28},{4,0},{8,4},{12,8},{16,12},{20,16},{24,20},{28,24},{1,29},{... | collective-permute-start | bytes 1572872 | tf_op jit(solution)/shard_map/ppermute | solution.py:104
  169.7 132.2 %collective-permute-start.3 = (bf16[256,3072]{1,0:T(8,128)(2,1)S(1)}, bf16[256,3072]{1,0:T(8,128)(2,1)}, u32[]{:S(2)}, u32[]{:S(2)}) collective-permute-start(bf16[256,3072]{1,0:T(8,128)(2,1)S(1)} %bitcast.255), channel_id=1, source_target_pairs={{0,28},{4,0},{8,4},{12,8},{16,12},{20,16},{24,20},{28,24},{1,29},{... | collective-permute-start | bytes 4718600 | tf_op jit(solution)/shard_map/ppermute | solution.py:104
  174.0 174.3 %collective-permute-start.4 = (bf16[256,3072]{1,0:T(8,128)(2,1)}, bf16[256,3072]{1,0:T(8,128)(2,1)}, u32[]{:S(2)}, u32[]{:S(2)}) collective-permute-start(bf16[256,3072]{1,0:T(8,128)(2,1)} %collective-permute-done.2), channel_id=1, source_target_pairs={{0,4},{4,8},{8,12},{12,16},{16,20},{20,24},{24,28},{28,0},{1,5},{5... | collective-permute-start | bytes 4718600 | tf_op jit(solution)/shard_map/ppermute | solution.py:97
  214.6 63.9 %collective-permute-start.12 = (bf16[128,2048]{1,0:T(8,128)(2,1)}, bf16[128,2048]{1,0:T(8,128)(2,1)}, u32[]{:S(2)}, u32[]{:S(2)}) collective-permute-start(bf16[128,2048]{1,0:T(8,128)(2,1)} %collective-permute-done.10), channel_id=1, source_target_pairs={{0,4},{4,8},{8,12},{12,16},{16,20},{20,24},{24,28},{28,0},{1,5},{5... | collective-permute-start | bytes 1572872 | tf_op jit(solution)/shard_map/ppermute | solution.py:97
  222.3 71.0 %collective-permute-start.33 = (bf16[128,2048]{1,0:T(8,128)(2,1)S(1)}, bf16[128,2048]{1,0:T(8,128)(2,1)S(1)}, u32[]{:S(2)}, u32[]{:S(2)}) collective-permute-start(bf16[128,2048]{1,0:T(8,128)(2,1)S(1)} %collective-permute-done.31), channel_id=1, source_target_pairs={{0,28},{4,0},{8,4},{12,8},{16,12},{20,16},{24,20},{28,24},{1,29},{... | collective-permute-start | bytes 1572872 | tf_op jit(solution)/shard_map/ppermute | solution.py:104
  237.1 63.9 %collective-permute-start.32 = (bf16[128,2048]{1,0:T(8,128)(2,1)}, bf16[128,2048]{1,0:T(8,128)(2,1)}, u32[]{:S(2)}, u32[]{:S(2)}) collective-permute-start(bf16[128,2048]{1,0:T(8,128)(2,1)} %collective-permute-done.30), channel_id=1, source_target_pairs={{0,4},{4,8},{8,12},{12,16},{16,20},{20,24},{24,28},{28,0},{1,5},{5... | collective-permute-start | bytes 1572872 | tf_op jit(solution)/shard_map/ppermute | solution.py:97
  243.2 57.7 %copy-start.46 = (bf16[2,256,2048]{2,1,0:T(8,128)(2,1)S(1)}, bf16[2,256,2048]{2,1,0:T(8,128)(2,1)}, u32[]{:S(2)}) copy-start(bf16[2,256,2048]{2,1,0:T(8,128)(2,1)} %maximum_select_fusion.4) | copy-start | bytes 6291460
  278.5 37.3 %collective-permute-start.15 = (bf16[128,2048]{1,0:T(8,128)(2,1)S(1)}, bf16[128,2048]{1,0:T(8,128)(2,1)S(1)}, u32[]{:S(2)}, u32[]{:S(2)}) collective-permute-start(bf16[128,2048]{1,0:T(8,128)(2,1)S(1)} %collective-permute-done.13), channel_id=1, source_target_pairs={{0,28},{4,0},{8,4},{12,8},{16,12},{20,16},{24,20},{28,24},{1,29},{... | collective-permute-start | bytes 1572872 | tf_op jit(solution)/shard_map/ppermute | solution.py:104
  293.3 52.6 %collective-permute-start.14 = (bf16[128,2048]{1,0:T(8,128)(2,1)}, bf16[128,2048]{1,0:T(8,128)(2,1)S(1)}, u32[]{:S(2)}, u32[]{:S(2)}) collective-permute-start(bf16[128,2048]{1,0:T(8,128)(2,1)} %collective-permute-done.12), channel_id=1, source_target_pairs={{0,4},{4,8},{8,12},{12,16},{16,20},{20,24},{24,28},{28,0},{1,5},{5... | collective-permute-start | bytes 1572872 | tf_op jit(solution)/shard_map/ppermute | solution.py:97
  300.9 109.0 %collective-permute-start.1 = (bf16[2,256,2048]{2,1,0:T(8,128)(2,1)S(1)}, bf16[2,256,2048]{2,1,0:T(8,128)(2,1)S(1)}, u32[]{:S(2)}, u32[]{:S(2)}) collective-permute-start(bf16[2,256,2048]{2,1,0:T(8,128)(2,1)S(1)} %copy-done.46), channel_id=1, source_target_pairs={{0,1},{1,0},{2,3},{3,2},{4,5},{5,4},{6,7},{7,6},{8,9},{9,8},{10,11... | collective-permute-start | bytes 6291464 | tf_op jit(solution)/shard_map/ppermute | solution.py:55
  301.8 103.2 %collective-permute-start.5 = (bf16[256,3072]{1,0:T(8,128)(2,1)}, bf16[256,3072]{1,0:T(8,128)(2,1)S(1)}, u32[]{:S(2)}, u32[]{:S(2)}) collective-permute-start(bf16[256,3072]{1,0:T(8,128)(2,1)} %collective-permute-done.3), channel_id=1, source_target_pairs={{0,28},{4,0},{8,4},{12,8},{16,12},{20,16},{24,20},{28,24},{1,29},{... | collective-permute-start | bytes 4718600 | tf_op jit(solution)/shard_map/ppermute | solution.py:104
  315.7 41.4 %collective-permute-start.34 = (bf16[128,2048]{1,0:T(8,128)(2,1)}, bf16[128,2048]{1,0:T(8,128)(2,1)S(1)}, u32[]{:S(2)}, u32[]{:S(2)}) collective-permute-start(bf16[128,2048]{1,0:T(8,128)(2,1)} %collective-permute-done.32), channel_id=1, source_target_pairs={{0,4},{4,8},{8,12},{12,16},{16,20},{20,24},{24,28},{28,0},{1,5},{5... | collective-permute-start | bytes 1572872 | tf_op jit(solution)/shard_map/ppermute | solution.py:97
  345.9 22.4 %collective-permute-start.16 = (bf16[128,2048]{1,0:T(8,128)(2,1)S(1)}, bf16[128,2048]{1,0:T(8,128)(2,1)S(1)}, u32[]{:S(2)}, u32[]{:S(2)}) collective-permute-start(bf16[128,2048]{1,0:T(8,128)(2,1)S(1)} %collective-permute-done.14), channel_id=1, source_target_pairs={{0,4},{4,8},{8,12},{12,16},{16,20},{20,24},{24,28},{28,0},{1,5},{5... | collective-permute-start | bytes 1572872 | tf_op jit(solution)/shard_map/ppermute | solution.py:97
  348.3 60.0 %collective-permute-start.6 = (bf16[256,3072]{1,0:T(8,128)(2,1)}, bf16[256,3072]{1,0:T(8,128)(2,1)S(1)}, u32[]{:S(2)}, u32[]{:S(2)}) collective-permute-start(bf16[256,3072]{1,0:T(8,128)(2,1)} %collective-permute-done.4), channel_id=1, source_target_pairs={{0,4},{4,8},{8,12},{12,16},{16,20},{20,24},{24,28},{28,0},{1,5},{5... | collective-permute-start | bytes 4718600 | tf_op jit(solution)/shard_map/ppermute | solution.py:97
  405.0 69.5 %collective-permute-start.7 = (bf16[256,3072]{1,0:T(8,128)(2,1)S(1)}, bf16[256,3072]{1,0:T(8,128)(2,1)S(1)}, u32[]{:S(2)}, u32[]{:S(2)}) collective-permute-start(bf16[256,3072]{1,0:T(8,128)(2,1)S(1)} %collective-permute-done.5), channel_id=1, source_target_pairs={{0,28},{4,0},{8,4},{12,8},{16,12},{20,16},{24,20},{28,24},{1,29},{... | collective-permute-start | bytes 4718600 | tf_op jit(solution)/shard_map/ppermute | solution.py:104
  408.2 66.5 %collective-permute-start.8 = (bf16[256,3072]{1,0:T(8,128)(2,1)S(1)}, bf16[256,3072]{1,0:T(8,128)(2,1)}, u32[]{:S(2)}, u32[]{:S(2)}) collective-permute-start(bf16[256,3072]{1,0:T(8,128)(2,1)S(1)} %collective-permute-done.6), channel_id=1, source_target_pairs={{0,4},{4,8},{8,12},{12,16},{16,20},{20,24},{24,28},{28,0},{1,5},{5... | collective-permute-start | bytes 4718600 | tf_op jit(solution)/shard_map/ppermute | solution.py:97
  414.5 61.8 %copy-start.31 = (bf16[2,2,256,2048]{3,2,1,0:T(8,128)(2,1)}, bf16[2,2,256,2048]{3,2,1,0:T(8,128)(2,1)S(1)}, u32[]{:S(2)}) copy-start(bf16[2,2,256,2048]{3,2,1,0:T(8,128)(2,1)S(1)} %copy.197) | copy-start | bytes 12582916
  556.1 4.3 collective-permute-start.17
  566.0 56.0 %collective-permute-start.18 = (bf16[1,256,2048]{2,1,0:T(8,128)(2,1)S(1)}, bf16[1,256,2048]{2,1,0:T(8,128)(2,1)}, u32[]{:S(2)}, u32[]{:S(2)}) collective-permute-start(bf16[1,256,2048]{2,1,0:T(8,128)(2,1)S(1)} %dynamic-slice_convert_fusion.4), channel_id=1, source_target_pairs={{0,2},{1,3},{2,0},{3,1},{4,6},{5,7},{6,4},{7,5},{8,10},{9,11},{10,... | collective-permute-start | bytes 3145736 | tf_op jit(solution)/shard_map/ppermute | solution.py:55
  596.9 22.5 %collective-permute-start.21 = (bf16[256,1024]{1,0:T(8,128)(2,1)S(1)}, bf16[256,1024]{1,0:T(8,128)(2,1)S(1)}, u32[]{:S(2)}, u32[]{:S(2)}) collective-permute-start(bf16[256,1024]{1,0:T(8,128)(2,1)S(1)} %bitcast.286), channel_id=1, source_target_pairs={{0,4},{4,8},{8,12},{12,16},{16,20},{20,24},{24,28},{28,0},{1,5},{5... | collective-permute-start | bytes 1572872 | tf_op jit(solution)/shard_map/ppermute | solution.py:97
  597.3 29.4 %collective-permute-start.37 = (bf16[1,256,2048]{2,1,0:T(8,128)(2,1)}, bf16[1,256,2048]{2,1,0:T(8,128)(2,1)S(1)}, u32[]{:S(2)}, u32[]{:S(2)}) collective-permute-start(bf16[1,256,2048]{2,1,0:T(8,128)(2,1)} %bitcast.42), channel_id=1, source_target_pairs={{0,2},{1,3},{2,0},{3,1},{4,6},{5,7},{6,4},{7,5},{8,10},{9,11},{10,... | collective-permute-start | bytes 3145736 | tf_op jit(solution)/shard_map/ppermute | solution.py:55
  598.7 29.9 %collective-permute-start.22 = (bf16[256,1024]{1,0:T(8,128)(2,1)S(1)}, bf16[256,1024]{1,0:T(8,128)(2,1)S(1)}, u32[]{:S(2)}, u32[]{:S(2)}) collective-permute-start(bf16[256,1024]{1,0:T(8,128)(2,1)S(1)} %bitcast.287), channel_id=1, source_target_pairs={{0,28},{4,0},{8,4},{12,8},{16,12},{20,16},{24,20},{28,24},{1,29},{... | collective-permute-start | bytes 1572872 | tf_op jit(solution)/shard_map/ppermute | solution.py:104
  619.4 25.3 %collective-permute-start.23 = (bf16[256,1024]{1,0:T(8,128)(2,1)S(1)}, bf16[256,1024]{1,0:T(8,128)(2,1)S(1)}, u32[]{:S(2)}, u32[]{:S(2)}) collective-permute-start(bf16[256,1024]{1,0:T(8,128)(2,1)S(1)} %collective-permute-done.21), channel_id=1, source_target_pairs={{0,4},{4,8},{8,12},{12,16},{16,20},{20,24},{24,28},{28,0},{1,5},{5... | collective-permute-start | bytes 1572872 | tf_op jit(solution)/shard_map/ppermute | solution.py:97
  625.2 35.2 %collective-permute-start.19 = (bf16[1,256,2048]{2,1,0:T(8,128)(2,1)S(1)}, bf16[1,256,2048]{2,1,0:T(8,128)(2,1)S(1)}, u32[]{:S(2)}, u32[]{:S(2)}) collective-permute-start(bf16[1,256,2048]{2,1,0:T(8,128)(2,1)S(1)} %fusion.126), channel_id=1, source_target_pairs={{0,2},{1,3},{2,0},{3,1},{4,6},{5,7},{6,4},{7,5},{8,10},{9,11},{10,... | collective-permute-start | bytes 3145736 | tf_op jit(solution)/shard_map/ppermute | solution.py:55
  628.5 55.1 %collective-permute-start.38 = (bf16[2,256,2048]{2,1,0:T(8,128)(2,1)S(1)}, bf16[2,256,2048]{2,1,0:T(8,128)(2,1)S(1)}, u32[]{:S(2)}, u32[]{:S(2)}) collective-permute-start(bf16[2,256,2048]{2,1,0:T(8,128)(2,1)S(1)} %maximum_select_fusion.8), channel_id=1, source_target_pairs={{0,1},{1,0},{2,3},{3,2},{4,5},{5,4},{6,7},{7,6},{8,9},{9,8},{10,11... | collective-permute-start | bytes 6291464 | tf_op jit(solution)/shard_map/ppermute | solution.py:55
  628.6 29.7 %collective-permute-start.24 = (bf16[256,1024]{1,0:T(8,128)(2,1)S(1)}, bf16[256,1024]{1,0:T(8,128)(2,1)S(1)}, u32[]{:S(2)}, u32[]{:S(2)}) collective-permute-start(bf16[256,1024]{1,0:T(8,128)(2,1)S(1)} %collective-permute-done.22), channel_id=1, source_target_pairs={{0,28},{4,0},{8,4},{12,8},{16,12},{20,16},{24,20},{28,24},{1,29},{... | collective-permute-start | bytes 1572872 | tf_op jit(solution)/shard_map/ppermute | solution.py:104
  644.7 13.7 collective-permute-start.25
  658.3 25.1 %collective-permute-start.26 = (bf16[256,1024]{1,0:T(8,128)(2,1)S(1)}, bf16[256,1024]{1,0:T(8,128)(2,1)S(1)}, u32[]{:S(2)}, u32[]{:S(2)}) collective-permute-start(bf16[256,1024]{1,0:T(8,128)(2,1)S(1)} %collective-permute-done.24), channel_id=1, source_target_pairs={{0,28},{4,0},{8,4},{12,8},{16,12},{20,16},{24,20},{28,24},{1,29},{... | collective-permute-start | bytes 1572872 | tf_op jit(solution)/shard_map/ppermute | solution.py:104
  658.4 25.2 %collective-permute-start.27 = (bf16[256,1024]{1,0:T(8,128)(2,1)S(1)}, bf16[256,1024]{1,0:T(8,128)(2,1)S(1)}, u32[]{:S(2)}, u32[]{:S(2)}) collective-permute-start(bf16[256,1024]{1,0:T(8,128)(2,1)S(1)} %collective-permute-done.25), channel_id=1, source_target_pairs={{0,4},{4,8},{8,12},{12,16},{16,20},{20,24},{24,28},{28,0},{1,5},{5... | collective-permute-start | bytes 1572872 | tf_op jit(solution)/shard_map/ppermute | solution.py:97
  660.7 25.0 %collective-permute-start.20 = (bf16[2,256,2048]{2,1,0:T(8,128)(2,1)S(1)}, bf16[2,256,2048]{2,1,0:T(8,128)(2,1)S(1)}, u32[]{:S(2)}, u32[]{:S(2)}) collective-permute-start(bf16[2,256,2048]{2,1,0:T(8,128)(2,1)S(1)} %maximum_select_fusion.6), channel_id=1, source_target_pairs={{0,1},{1,0},{2,3},{3,2},{4,5},{5,4},{6,7},{7,6},{8,9},{9,8},{10,11... | collective-permute-start | bytes 6291464 | tf_op jit(solution)/shard_map/ppermute | solution.py:55
  729.5 225.8 %reduce-scatter.14.cloned.1.call-start = ((), (), s32[]{:S(2)}) async-start(), calls=%async_computation.12 | async-start | bytes 4718592 | tf_op jit(solution)/shard_map/reduce_scatter | solution.py:116
  732.3 7.5 collective-permute-start.39
  739.6 4.2 collective-permute-start.35
  742.5 26.0 %collective-permute-start.40 = (bf16[1,256,2048]{2,1,0:T(8,128)(2,1)S(1)}, bf16[1,256,2048]{2,1,0:T(8,128)(2,1)S(1)}, u32[]{:S(2)}, u32[]{:S(2)}) collective-permute-start(bf16[1,256,2048]{2,1,0:T(8,128)(2,1)S(1)} %dynamic-slice_convert_fusion.2), channel_id=1, source_target_pairs={{0,2},{1,3},{2,0},{3,1},{4,6},{5,7},{6,4},{7,5},{8,10},{9,11},{10,... | collective-permute-start | bytes 3145736 | tf_op jit(solution)/shard_map/ppermute | solution.py:55
  744.8 45.6 %collective-permute-start.36 = (bf16[1,256,2048]{2,1,0:T(8,128)(2,1)S(1)}, bf16[1,256,2048]{2,1,0:T(8,128)(2,1)S(1)}, u32[]{:S(2)}, u32[]{:S(2)}) collective-permute-start(bf16[1,256,2048]{2,1,0:T(8,128)(2,1)S(1)} %dynamic-slice_convert_fusion.3), channel_id=1, source_target_pairs={{0,2},{1,3},{2,0},{3,1},{4,6},{5,7},{6,4},{7,5},{8,10},{9,11},{10,... | collective-permute-start | bytes 3145736 | tf_op jit(solution)/shard_map/ppermute | solution.py:55
  794.7 24.7 %collective-permute-start.41 = (bf16[1,256,2048]{2,1,0:T(8,128)(2,1)S(1)}, bf16[1,256,2048]{2,1,0:T(8,128)(2,1)S(1)}, u32[]{:S(2)}, u32[]{:S(2)}) collective-permute-start(bf16[1,256,2048]{2,1,0:T(8,128)(2,1)S(1)} %fusion.124), channel_id=1, source_target_pairs={{0,2},{1,3},{2,0},{3,1},{4,6},{5,7},{6,4},{7,5},{8,10},{9,11},{10,... | collective-permute-start | bytes 3145736 | tf_op jit(solution)/shard_map/ppermute | solution.py:55
  821.1 9.8 collective-permute-start.42
  827.4 296.8 %reduce-scatter.8.cloned.1.call-start = ((), (), s32[]{:S(2)}) async-start(), calls=%async_computation.9 | async-start | bytes 14155776 | tf_op jit(solution)/shard_map/reduce_scatter | solution.py:116
  906.9 308.1 %reduce-scatter.10.cloned.1.call-start = ((), (), s32[]{:S(2)}) async-start(), calls=%async_computation.10 | async-start | bytes 4718592 | tf_op jit(solution)/shard_map/reduce_scatter | solution.py:116
  940.5 4.3 collective-permute-start.43
  948.9 36.9 %collective-permute-start.44 = (bf16[1,256,2048]{2,1,0:T(8,128)(2,1)}, bf16[1,256,2048]{2,1,0:T(8,128)(2,1)}, u32[]{:S(2)}, u32[]{:S(2)}) collective-permute-start(bf16[1,256,2048]{2,1,0:T(8,128)(2,1)} %dynamic-slice_convert_fusion.1), channel_id=1, source_target_pairs={{0,2},{1,3},{2,0},{3,1},{4,6},{5,7},{6,4},{7,5},{8,10},{9,11},{10,... | collective-permute-start | bytes 3145736 | tf_op jit(solution)/shard_map/ppermute | solution.py:55
  948.9 31.4 %all-to-all-start.3 = ((bf16[4,64,1024]{2,1,0:T(8,128)(2,1)}), bf16[4,64,1024]{2,1,0:T(8,128)(2,1)}, u32[]{:S(2)}, u32[]{:S(2)}) async-start(bf16[4,64,1024]{2,1,0:T(8,128)(2,1)} %bitcast.296), calls=%async_computation.6 | async-start | bytes 1048576 | tf_op jit(solution)/shard_map/all_to_all | solution.py:84
  953.0 399.3 %reduce-scatter.16.cloned.1.call-start = ((), (), s32[]{:S(2)}) async-start(), calls=%async_computation.13 | async-start | bytes 1081344
  1124.3 232.4 %all-to-all-start.2 = ((bf16[4,64,3072]{2,1,0:T(8,128)(2,1)}), bf16[4,64,3072]{2,1,0:T(8,128)(2,1)}, u32[]{:S(2)}, u32[]{:S(2)}) async-start(bf16[4,64,3072]{2,1,0:T(8,128)(2,1)} %bitcast.293), calls=%async_computation.3 | async-start | bytes 3145728 | tf_op jit(solution)/shard_map/all_to_all | solution.py:84
  1215.0 140.7 %collective-permute-start.45 = (bf16[128,2048]{1,0:T(8,128)(2,1)}, bf16[128,2048]{1,0:T(8,128)(2,1)S(1)}, u32[]{:S(2)}, u32[]{:S(2)}) collective-permute-start(bf16[128,2048]{1,0:T(8,128)(2,1)} %reduce-scatter.10.cloned.1.call-done), channel_id=1, source_target_pairs={{0,0},{4,1},{8,2},{12,3},{16,4},{20,5},{24,6},{28,7},{1,8},{5,9},{... | collective-permute-start | bytes 1572872 | tf_op jit(solution)/shard_map/ppermute | solution.py:231
  (76 other events, 506.6 us)
Sparse Core Ops, SparseCore 0:
  729.7 85.7 reduce-scatter.11
  827.6 85.9 reduce-scatter.13
  917.2 207.0 reduce-scatter.7
  1127.8 87.1 reduce-scatter.9
  1217.7 134.5 reduce-scatter.15
